TPU v7x, 256 devices: a whole 4x4x8 slice. The times are simulated.
256 devices in a mesh: band: 4 (over x_hi, core), grid: 64 (over x_lo, z, y).
Axes of the slice: x: 4 (x_hi: 2, x_lo: 2; x = x_hi * 2 + x_lo), y: 4, z: 8, core: 2. Of those that a mesh axis runs over, the one named last changes fastest.
Arguments:
- orbitals: float32 [768, 16, 16, 512], P('grid', None, None, 'band'), may hold values from -24 to 24
- potential: float32 [768, 16, 16], P('grid'), may hold values from -3 to -1
- projectors: float32 [256, 8, 13, 256], P('grid'), may hold values from -0.109375 to 0.109375
- atom_planes: int32 [256, 13], P('grid'), may hold values from 0 to 23, as said below
- kb_energy: float32 [8], replicated, may hold values from 1 to 4
Outputs:
- filtered: float32 [768, 16, 16, 512], P('grid', None, None, 'band')
- correlation_gram: float32 [512, 512], P('band')
Inputs may be any that keep to these rules, and one draw needn't show every extreme that they name: `atom_planes`: each atom's row holds 13 consecutive plane numbers; the first atom starts at plane 0 and the last atom at plane 12 - 1.
All inputs are finite; a program needn't handle non-finite values.
Results may differ from a plain program's by a relative error of at most 0.0003.
Values sent between devices are 32-bit elements; how exact they have to be, the bound alone decides.
A program may use at most 128 MiB of HBM per device.

v0:
```python
import jax
import jax.numpy as jnp
from jax import lax
from jax.sharding import PartitionSpec as P

DEGREE = 4
WEIGHTS = (
    -5369.0 / 1800.0,
    12.0 / 7.0,
    -15.0 / 56.0,
    10.0 / 189.0,
    -1.0 / 112.0,
    2.0 / 1925.0,
    -1.0 / 16632.0,
)
LOWER = -4.0
CUTOFF = 1.0
UPPER = 16.0
PRECISE = lax.Precision.HIGHEST


def padded(array, sides, width):
    for axis, dim in sides:
        peers, length = (lax.axis_size(axis), array.shape[dim])
        up = [(i, (i + 1) % peers) for i in range(peers)]
        down = [(j, i) for i, j in up]
        last = lax.slice_in_dim(array, length - width, length, axis=dim)
        initial = lax.slice_in_dim(array, 0, width, axis=dim)
        before = lax.ppermute(last, axis, up)
        after = lax.ppermute(initial, axis, down)
        array = jnp.concatenate([before, array, after], axis=dim)
    return array


def shifted(array, axis, by):
    peers = lax.axis_size(axis)
    return lax.ppermute(array, axis, [(i, (i + by) % peers) for i in range(peers)])


def filter_terms(degree):
    half_span = (UPPER - CUTOFF) / 2.0
    middle = (UPPER + CUTOFF) / 2.0
    sigma_now = half_span / (LOWER - middle)
    sigma_first = sigma_now
    scales = [sigma_now / half_span]
    recall = [0.0]
    for level in range(1, degree):
        sigma_next = 1.0 / (2.0 / sigma_first - sigma_now)
        scales.append(2.0 * sigma_next / half_span)
        recall.append(sigma_now * sigma_next)
        sigma_now = sigma_next
    return (middle, scales, recall)


def second_roll(values, along):
    summed = WEIGHTS[0] * values
    for reach in range(1, 7):
        summed = summed + WEIGHTS[reach] * (
            jnp.roll(values, reach, along) + jnp.roll(values, -reach, along)
        )
    return summed


def second_planes(widened, slab_planes):
    summed = WEIGHTS[0] * widened[6 : 6 + slab_planes]
    for reach in range(1, 7):
        summed = summed + WEIGHTS[reach] * (
            widened[6 + reach : 6 + reach + slab_planes]
            + widened[6 - reach : 6 - reach + slab_planes]
        )
    return summed


def shards(orbitals, potential, projectors, atom_planes, kb_energy):
    slab_planes = orbitals.shape[0]
    orb_here = orbitals.shape[-1]
    extent = slab_planes + 12
    atom_count = atom_planes.shape[0]
    plane_marks = (
        atom_planes[:, :, None] == jnp.arange(extent, dtype=jnp.int32)[None, None, :]
    ).astype(jnp.float32)
    projector_map = jnp.einsum("abe,apbs->apes", plane_marks, projectors, precision=PRECISE)
    map_rows = atom_count * projectors.shape[1]
    projector_map = projector_map.reshape(map_rows, -1)
    energy_col = jnp.tile(kb_energy, atom_count)[:, None]
    middle, scales, recall = filter_terms(DEGREE)
    previous = orbitals
    current = orbitals
    for level in range(DEGREE):
        widened = padded(current, (("grid", 0),), 6)
        lap = (
            second_planes(widened, slab_planes) + second_roll(current, 1) + second_roll(current, 2)
        )
        local_part = -0.5 * lap + potential[..., None] * current
        correlation = (
            jnp.dot(projector_map, widened.reshape(-1, orb_here), precision=PRECISE) * energy_col
        )
        spread = lax.dot_general(
            projector_map, correlation, (((0,), (0,)), ((), ())), precision=PRECISE
        )
        spread = spread.reshape(widened.shape)
        own_part = local_part + spread[6 : 6 + slab_planes]
        low_rim = spread[:6]
        high_rim = spread[6 + slab_planes :]
        from_below = shifted(high_rim, "grid", 1)
        from_above = shifted(low_rim, "grid", -1)
        applied = own_part.at[:6].add(from_below).at[slab_planes - 6 :].add(from_above)
        result = scales[level] * (applied - middle * current)
        if level > 0:
            result = result - recall[level] * previous
        previous = current
        current = result
    flattened = current.reshape(-1, orb_here)
    piece = lax.all_gather(current, "band", axis=3, tiled=True)
    gram_part = lax.dot_general(
        flattened, piece.reshape(-1, piece.shape[-1]), (((0,), (0,)), ((), ())), precision=PRECISE
    )
    gram_total = lax.psum(gram_part, "grid")
    cell_count = slab_planes * orbitals.shape[1] * orbitals.shape[2] * lax.axis_size("grid")
    correlation_gram = gram_total * (1.0 / cell_count)
    return (current, correlation_gram)


def solution(mesh):
    return jax.shard_map(
        shards,
        mesh=mesh,
        in_specs=(
            P("grid", None, None, "band"),
            P("grid", None, None),
            P("grid", None, None, None),
            P("grid", None),
            P(),
        ),
        out_specs=(P("grid", None, None, "band"), P("band", None)),
        check_vma=False,
    )
```

profile of v0, /device:TPU:4, one launch (start us, length us, event | category | flops | bytes accessed | tf_op | source)
XLA Modules:
  0.0 995.4 jit_solution(16665948579629088824)
XLA Ops:
  7.2 2.8 fusion.325
  11.6 7.4 collective-permute-start
  37.5 1.9 fusion.321
  39.3 1.8 fusion.323
  41.2 2.0 fusion.305
  43.2 2.0 fusion.307
  45.2 2.0 fusion.303
  47.2 2.0 fusion.309
  52.9 2.0 fusion.301
  54.8 2.0 fusion.311
  60.2 5.1 fusion.326
  70.2 6.2 collective-permute-start.3
  77.7 14.2 %fusion.105 = f32[12,16,16,128]{3,2,1,0:T(8,128)S(1)} fusion(f32[12,16,16,128]{3,2,1,0:T(8,128)S(1)} %bitcast.60, f32[18,16,16,128]{3,2,1,0:T(8,128)S(1)} %get-tuple-element.305, f32[18,16,16,128]{3,2,1,0:T(8,128)S(1)} %constant_dynamic-update-slice_fusion, f32[12,15,16,128]{3,2,1,0:T(8,128)} %get-tuple-element.301, ...), kind=kLoop, calls=%fused_computation.176 | loop fusion | flops 33423360 | bytes 61353984 | tf_op jit(solution)/shard_map/add | solution.py:102
  91.9 1.8 collective-permute-done.2
  114.5 1.9 fusion.296
  116.4 1.8 fusion.298
  118.3 2.1 fusion.282
  120.4 2.0 fusion.276
  122.4 2.1 fusion.284
  124.5 2.1 fusion.280
  126.6 6.4 collective-permute-start.4
  133.7 2.0 fusion.286
  135.7 2.0 fusion.278
  137.7 11.2 %collective-permute-done.5 = f32[6,16,16,128]{3,2,1,0:T(8,128)S(1)} collective-permute-done((f32[6,16,16,128]{3,2,1,0:T(8,128)S(1)}, f32[6,16,16,128]{3,2,1,0:T(8,128)S(1)}, u32[]{:S(2)}, u32[]{:S(2)}) %collective-permute-start.5) | collective-permute-done | bytes 786464 | tf_op jit(solution)/shard_map/ppermute | solution.py:29
  151.6 5.1 fusion.327
  159.2 6.6 collective-permute-start.7
  165.8 20.1 %fusion.71 = f32[12,16,16,128]{3,2,1,0:T(8,128)} fusion(f32[12,16,16,128]{3,2,1,0:T(8,128)} %bitcast.61, f32[12,16,16,128]{3,2,1,0:T(8,128)S(1)} %broadcast_multiply_fusion, f32[6,16,16,128]{3,2,1,0:T(8,128)S(1)} %collective-permute-done.5, f32[6,16,16,128]{3,2,1,0:T(8,128)} %copy-done.9, f32[12,15,16,128]{3,2,1,0:T(8,128)} %get-tuple-element.251, ...), kind=kLoop, calls=%fused_computation.135 | loop fusion | flops 38928384 | bytes 47198208 | tf_op jit(solution)/shard_map/add | solution.py:102
  185.9 2.4 fusion.215
  188.2 2.4 fusion.214
  190.6 1.9 multiply_subtract_fusion.2
  210.3 1.9 fusion.271
  212.2 1.8 fusion.273
  214.1 2.0 fusion.257
  216.1 2.0 fusion.253
  218.0 2.0 fusion.251
  220.0 2.0 fusion.259
  222.0 6.4 collective-permute-start.8
  229.1 2.0 fusion.261
  231.1 2.0 fusion.255
  233.1 9.9 collective-permute-done.9
  245.6 5.1 fusion.328
  252.1 6.4 collective-permute-start.11
  258.6 19.8 %fusion.40 = f32[12,16,16,128]{3,2,1,0:T(8,128)} fusion(f32[12,16,16,128]{3,2,1,0:T(8,128)S(1)} %bitcast.62, f32[12,16,16,128]{3,2,1,0:T(8,128)S(1)} %multiply_subtract_fusion.2, f32[6,16,16,128]{3,2,1,0:T(8,128)S(1)} %collective-permute-done.9, f32[6,16,16,128]{3,2,1,0:T(8,128)} %copy-done.11, f32[12,15,16,128]{3,2,1,0:T(8,128)} %get-tuple-element.201, ...), kind=kLoop, calls=%fused_computation.104 | loop fusion | flops 38141952 | bytes 44052480 | tf_op jit(solution)/shard_map/add | solution.py:102
  278.4 2.3 fusion.213
  280.7 2.4 fusion.212
  283.1 2.0 multiply_subtract_fusion.1
  299.8 1.8 fusion.242
  301.6 1.8 fusion.244
  303.4 1.9 fusion.246
  305.2 1.9 fusion.248
  307.1 2.0 fusion.232
  309.2 2.0 fusion.226
  311.2 2.0 fusion.234
  313.2 2.0 fusion.230
  315.2 6.6 collective-permute-start.12
  322.6 2.0 fusion.236
  324.6 2.0 fusion.228
  326.6 8.2 collective-permute-done.13
  337.4 5.1 fusion.329
  343.9 6.5 collective-permute-start.15
  350.4 18.8 %fusion.9 = f32[12,16,16,128]{3,2,1,0:T(8,128)S(1)} fusion(f32[12,16,16,128]{3,2,1,0:T(8,128)S(1)} %bitcast.63, f32[12,16,16,128]{3,2,1,0:T(8,128)S(1)} %multiply_subtract_fusion.1, f32[6,16,16,128]{3,2,1,0:T(8,128)S(1)} %collective-permute-done.13, f32[6,16,16,128]{3,2,1,0:T(8,128)} %copy-done.10, f32[12,15,16,128]{3,2,1,0:T(8,128)} %get-tuple-element.151, ...), kind=kLoop, calls=%fused_computation.73 | loop fusion | flops 38141952 | bytes 44052480 | tf_op jit(solution)/shard_map/add | solution.py:102
  373.4 45.7 %all-gather.2.cloned.1.call-done = f32[12,16,16,512]{3,2,1,0:T(8,128)} async-done(((f32[12,16,16,128]{3,2,1,0:T(8,128)}), f32[12,16,16,512]{3,2,1,0:T(8,128)}) %all-gather.2.cloned.1.call-update) | async-done | bytes 6291472 | tf_op jit(solution)/shard_map/all_gather | solution.py:114
  419.2 7.4 convolution_bitcast_fusion.1
  426.6 560.1 %all-reduce.2.cloned.1.call-done = f32[128,512]{1,0:T(8,128)} async-done(((f32[128,512]{1,0:T(8,128)}), f32[128,512]{1,0:T(8,128)}) %all-reduce.2.cloned.1.call-update) | async-done | bytes 262160 | tf_op jit(solution)/shard_map/psum | solution.py:118
  (155 shorter events, 107.7 us)
Async XLA Ops:
  7.2 42.1 %copy-start = (f32[4,8,13,256]{3,1,2,0:T(8,128)S(1)}, f32[4,8,13,256]{3,1,2,0:T(8,128)}, u32[]{:S(2)}) copy-start(f32[4,8,13,256]{3,1,2,0:T(8,128)} %param.23) | copy-start | bytes 1277956
  7.2 11.8 %copy-start.2 = (f32[12,16,16,128]{3,2,1,0:T(8,128)S(1)}, f32[12,16,16,128]{3,2,1,0:T(8,128)}, u32[]{:S(2)}) copy-start(f32[12,16,16,128]{3,2,1,0:T(8,128)} %param.21) | copy-start | bytes 4718596
  7.2 412.0 %all-gather.2.cloned.1.call-start = ((), (), s32[]{:S(2)}) async-start(), calls=%async_computation | async-start | bytes 7864320 | tf_op jit(solution)/shard_map/all_gather | solution.py:114
  10.0 46.8 %collective-permute-start.1 = (f32[6,16,16,128]{3,2,1,0:T(8,128)}, f32[6,16,16,128]{3,2,1,0:T(8,128)}, u32[]{:S(2)}, u32[]{:S(2)}) collective-permute-start(f32[6,16,16,128]{3,2,1,0:T(8,128)} %get-tuple-element.306), channel_id=1, source_target_pairs={{0,1},{1,2},{2,3},{3,4},{4,5},{5,6},{6,7},{7,8},{8,9},{9,10},{10,1... | collective-permute-start | bytes 2359304 | tf_op jit(solution)/shard_map/ppermute | solution.py:29
  11.6 45.2 %collective-permute-start = (f32[6,16,16,128]{3,2,1,0:T(8,128)}, f32[6,16,16,128]{3,2,1,0:T(8,128)}, u32[]{:S(2)}, u32[]{:S(2)}) collective-permute-start(f32[6,16,16,128]{3,2,1,0:T(8,128)} %get-tuple-element.307), channel_id=1, source_target_pairs={{1,0},{2,1},{3,2},{4,3},{5,4},{6,5},{7,6},{8,7},{9,8},{10,9},{11,1... | collective-permute-start | bytes 2359304 | tf_op jit(solution)/shard_map/ppermute | solution.py:30
  47.2 2.1 copy-start.15
  47.2 3.6 copy-start.14
  47.2 4.2 copy-start.16
  65.3 1.7 copy-start.4
  68.3 9.3 copy-start.12
  68.3 9.3 copy-start.13
  69.6 8.1 copy-start.5
  69.6 8.1 copy-start.6
  69.6 8.1 copy-start.7
  70.1 7.6 slice-start
  70.1 23.6 %collective-permute-start.2 = (f32[6,16,16,128]{3,2,1,0:T(8,128)}, f32[6,16,16,128]{3,2,1,0:T(8,128)}, u32[]{:S(2)}, u32[]{:S(2)}) collective-permute-start(f32[6,16,16,128]{3,2,1,0:T(8,128)} %bitcast.5), channel_id=1, source_target_pairs={{0,1},{1,2},{2,3},{3,4},{4,5},{5,6},{6,7},{7,8},{8,9},{9,10},{10,1... | collective-permute-start | bytes 2359304 | tf_op jit(solution)/shard_map/ppermute | solution.py:37
  70.2 24.9 %collective-permute-start.3 = (f32[6,16,16,128]{3,2,1,0:T(8,128)}, f32[6,16,16,128]{3,2,1,0:T(8,128)}, u32[]{:S(2)}, u32[]{:S(2)}) collective-permute-start(f32[6,16,16,128]{3,2,1,0:T(8,128)} %bitcast.6), channel_id=1, source_target_pairs={{0,63},{1,0},{2,1},{3,2},{4,3},{5,4},{6,5},{7,6},{8,7},{9,8},{10,9... | collective-permute-start | bytes 2359304 | tf_op jit(solution)/shard_map/ppermute | solution.py:37
  126.6 22.4 %collective-permute-start.5 = (f32[6,16,16,128]{3,2,1,0:T(8,128)S(1)}, f32[6,16,16,128]{3,2,1,0:T(8,128)S(1)}, u32[]{:S(2)}, u32[]{:S(2)}) collective-permute-start(f32[6,16,16,128]{3,2,1,0:T(8,128)S(1)} %get-tuple-element.254), channel_id=1, source_target_pairs={{0,1},{1,2},{2,3},{3,4},{4,5},{5,6},{6,7},{7,8},{8,9},{9,10},{10,1... | collective-permute-start | bytes 2359304 | tf_op jit(solution)/shard_map/ppermute | solution.py:29
  126.6 22.4 %collective-permute-start.4 = (f32[6,16,16,128]{3,2,1,0:T(8,128)S(1)}, f32[6,16,16,128]{3,2,1,0:T(8,128)S(1)}, u32[]{:S(2)}, u32[]{:S(2)}) collective-permute-start(f32[6,16,16,128]{3,2,1,0:T(8,128)S(1)} %get-tuple-element.255), channel_id=1, source_target_pairs={{1,0},{2,1},{3,2},{4,3},{5,4},{6,5},{7,6},{8,7},{9,8},{10,9},{11,1... | collective-permute-start | bytes 2359304 | tf_op jit(solution)/shard_map/ppermute | solution.py:30
  148.9 1.0 copy-start.9
  159.2 26.7 %collective-permute-start.6 = (f32[6,16,16,128]{3,2,1,0:T(8,128)}, f32[6,16,16,128]{3,2,1,0:T(8,128)}, u32[]{:S(2)}, u32[]{:S(2)}) collective-permute-start(f32[6,16,16,128]{3,2,1,0:T(8,128)} %bitcast.9), channel_id=1, source_target_pairs={{0,1},{1,2},{2,3},{3,4},{4,5},{5,6},{6,7},{7,8},{8,9},{9,10},{10,1... | collective-permute-start | bytes 2359304 | tf_op jit(solution)/shard_map/ppermute | solution.py:37
  159.2 29.1 %collective-permute-start.7 = (f32[6,16,16,128]{3,2,1,0:T(8,128)}, f32[6,16,16,128]{3,2,1,0:T(8,128)}, u32[]{:S(2)}, u32[]{:S(2)}) collective-permute-start(f32[6,16,16,128]{3,2,1,0:T(8,128)} %bitcast.10), channel_id=1, source_target_pairs={{0,63},{1,0},{2,1},{3,2},{4,3},{5,4},{6,5},{7,6},{8,7},{9,8},{10,9... | collective-permute-start | bytes 2359304 | tf_op jit(solution)/shard_map/ppermute | solution.py:37
  222.0 20.9 %collective-permute-start.9 = (f32[6,16,16,128]{3,2,1,0:T(8,128)S(1)}, f32[6,16,16,128]{3,2,1,0:T(8,128)S(1)}, u32[]{:S(2)}, u32[]{:S(2)}) collective-permute-start(f32[6,16,16,128]{3,2,1,0:T(8,128)S(1)} %get-tuple-element.204), channel_id=1, source_target_pairs={{0,1},{1,2},{2,3},{3,4},{4,5},{5,6},{6,7},{7,8},{8,9},{9,10},{10,1... | collective-permute-start | bytes 2359304 | tf_op jit(solution)/shard_map/ppermute | solution.py:29
  222.0 20.9 %collective-permute-start.8 = (f32[6,16,16,128]{3,2,1,0:T(8,128)S(1)}, f32[6,16,16,128]{3,2,1,0:T(8,128)S(1)}, u32[]{:S(2)}, u32[]{:S(2)}) collective-permute-start(f32[6,16,16,128]{3,2,1,0:T(8,128)S(1)} %get-tuple-element.205), channel_id=1, source_target_pairs={{1,0},{2,1},{3,2},{4,3},{5,4},{6,5},{7,6},{8,7},{9,8},{10,9},{11,1... | collective-permute-start | bytes 2359304 | tf_op jit(solution)/shard_map/ppermute | solution.py:30
  243.0 0.9 copy-start.11
  252.1 26.2 %collective-permute-start.10 = (f32[6,16,16,128]{3,2,1,0:T(8,128)}, f32[6,16,16,128]{3,2,1,0:T(8,128)}, u32[]{:S(2)}, u32[]{:S(2)}) collective-permute-start(f32[6,16,16,128]{3,2,1,0:T(8,128)} %bitcast.13), channel_id=1, source_target_pairs={{0,1},{1,2},{2,3},{3,4},{4,5},{5,6},{6,7},{7,8},{8,9},{9,10},{10,1... | collective-permute-start | bytes 2359304 | tf_op jit(solution)/shard_map/ppermute | solution.py:37
  252.1 28.6 %collective-permute-start.11 = (f32[6,16,16,128]{3,2,1,0:T(8,128)}, f32[6,16,16,128]{3,2,1,0:T(8,128)}, u32[]{:S(2)}, u32[]{:S(2)}) collective-permute-start(f32[6,16,16,128]{3,2,1,0:T(8,128)} %bitcast.14), channel_id=1, source_target_pairs={{0,63},{1,0},{2,1},{3,2},{4,3},{5,4},{6,5},{7,6},{8,7},{9,8},{10,9... | collective-permute-start | bytes 2359304 | tf_op jit(solution)/shard_map/ppermute | solution.py:37
  315.2 19.5 %collective-permute-start.13 = (f32[6,16,16,128]{3,2,1,0:T(8,128)S(1)}, f32[6,16,16,128]{3,2,1,0:T(8,128)S(1)}, u32[]{:S(2)}, u32[]{:S(2)}) collective-permute-start(f32[6,16,16,128]{3,2,1,0:T(8,128)S(1)} %get-tuple-element.154), channel_id=1, source_target_pairs={{0,1},{1,2},{2,3},{3,4},{4,5},{5,6},{6,7},{7,8},{8,9},{9,10},{10,1... | collective-permute-start | bytes 2359304 | tf_op jit(solution)/shard_map/ppermute | solution.py:29
  315.2 19.5 %collective-permute-start.12 = (f32[6,16,16,128]{3,2,1,0:T(8,128)S(1)}, f32[6,16,16,128]{3,2,1,0:T(8,128)S(1)}, u32[]{:S(2)}, u32[]{:S(2)}) collective-permute-start(f32[6,16,16,128]{3,2,1,0:T(8,128)S(1)} %get-tuple-element.155), channel_id=1, source_target_pairs={{1,0},{2,1},{3,2},{4,3},{5,4},{6,5},{7,6},{8,7},{9,8},{10,9},{11,1... | collective-permute-start | bytes 2359304 | tf_op jit(solution)/shard_map/ppermute | solution.py:30
  334.8 0.9 copy-start.10
  342.6 7.7 copy-start.8
  343.9 25.3 %collective-permute-start.14 = (f32[6,16,16,128]{3,2,1,0:T(8,128)}, f32[6,16,16,128]{3,2,1,0:T(8,128)}, u32[]{:S(2)}, u32[]{:S(2)}) collective-permute-start(f32[6,16,16,128]{3,2,1,0:T(8,128)} %bitcast.17), channel_id=1, source_target_pairs={{0,1},{1,2},{2,3},{3,4},{4,5},{5,6},{6,7},{7,8},{8,9},{9,10},{10,1... | collective-permute-start | bytes 2359304 | tf_op jit(solution)/shard_map/ppermute | solution.py:37
  343.9 26.7 %collective-permute-start.15 = (f32[6,16,16,128]{3,2,1,0:T(8,128)}, f32[6,16,16,128]{3,2,1,0:T(8,128)}, u32[]{:S(2)}, u32[]{:S(2)}) collective-permute-start(f32[6,16,16,128]{3,2,1,0:T(8,128)} %bitcast.18), channel_id=1, source_target_pairs={{0,63},{1,0},{2,1},{3,2},{4,3},{5,4},{6,5},{7,6},{8,7},{9,8},{10,9... | collective-permute-start | bytes 2359304 | tf_op jit(solution)/shard_map/ppermute | solution.py:37
  373.4 45.8 %copy-start.3 = (f32[12,16,16,128]{3,2,1,0:T(8,128)S(1)}, f32[12,16,16,128]{3,2,1,0:T(8,128)}, u32[]{:S(2)}) copy-start(f32[12,16,16,128]{3,2,1,0:T(8,128)} %multiply_subtract_fusion) | copy-start | bytes 4718596
  373.4 613.3 %all-reduce.2.cloned.1.call-start = ((), (), s32[]{:S(2)}) async-start(), calls=%async_computation.1 | async-start | bytes 524288 | tf_op jit(solution)/shard_map/psum | solution.py:118
  419.2 569.2 %copy-start.1 = (f32[4,8,13,256]{3,1,2,0:T(8,128)S(1)}, f32[4,8,13,256]{3,1,2,0:T(8,128)}, u32[]{:S(2)}) copy-start(f32[4,8,13,256]{3,1,2,0:T(8,128)} %param.23) | copy-start | bytes 1277956
Sparse Core Ops, SparseCore 0:
  373.5 45.6 all-gather.1
  426.7 559.9 all-reduce.1
where the time goes:
time: 1010 us; the launch traced here: 995 us
  waiting for transfers between devices  637 us (63%)
  local copies, waits for them, and re-layouts  155 us (15%)
  other arithmetic  98.3 us (10%)
  starting transfers between devices  54.4 us (5%)
  matrix products  36.1 us (4%)
  between operations  14.6 us (1%)
    psum x1, waiting for transfers between devices, shards(): gram_total = lax.psum(gram_part, 'grid')  560 us
    slice x96, local copies, waits for them, and re-layouts, second_roll(): jnp.roll(values, -reach, along)  137 us
    add x4, other arithmetic, shards(): own_part = local_part + spread[6:6 + slab_planes]  72.9 us
    all_gather x1, waiting for transfers between devices, shards(): piece = lax.all_gather(current, 'band', axis=3, tiled=True)  45.7 us
    ppermute x4, waiting for transfers between devices, padded(): before = lax.ppermute(last, axis, up)  29.3 us
    ppermute x4, starting transfers between devices, padded(): after = lax.ppermute(initial, axis, down)  26.8 us
    ppermute x8, starting transfers between devices, shifted(): lax.ppermute(array, axis, [(i, (i + by) % peers) for i in range(peers)])  25.9 us
    dot_general x4, matrix products, shards(): lax.dot_general(projector_map, correlation, (((0,), (0,)), ((), ())), pre...  20.3 us
  transfers between devices with their start and end apart: 18, of which 6 were waited for; matrix products, arithmetic and copies ran while one was open for 13% of the time, Pallas kernels for 0%

commit v1 on v0

--- a/solution.py
+++ b/solution.py
@@ -115,7 +115,7 @@
     gram_part = lax.dot_general(
         flattened, piece.reshape(-1, piece.shape[-1]), (((0,), (0,)), ((), ())), precision=PRECISE
     )
-    gram_total = lax.psum(gram_part, "grid")
+    gram_total = jnp.sum(lax.all_gather(gram_part, "grid"), axis=0)
     cell_count = slab_planes * orbitals.shape[1] * orbitals.shape[2] * lax.axis_size("grid")
     correlation_gram = gram_total * (1.0 / cell_count)
     return (current, correlation_gram)

time: 1010 us -> 781 us (0.77)
  waiting for transfers between devices: 637 us -> 406 us
    psum x1 -> x0, waiting for transfers between devices: 560 us -> none  [shards(): gram_total = lax.psum(gram_part, 'grid')]
    all_gather x0 -> x1, waiting for transfers between devices: none -> 329 us  [shards(): gram_total = jnp.sum(lax.all_gather(gram_part, 'grid'), axis=0)]
  transfers between devices with their start and end apart: 18 -> 18, of which waited for: 6 -> 6; matrix products, arithmetic and copies ran while one was open for 13% -> 17% of each run, Pallas kernels for 0% -> 0%
where the time goes in v1:
time: 781 us; the launch traced here: 771 us
  waiting for transfers between devices  406 us (52%)
  local copies, waits for them, and re-layouts  155 us (20%)
  other arithmetic  105 us (13%)
  starting transfers between devices  54.4 us (7%)
  matrix products  36.1 us (5%)
  between operations  14.6 us (2%)
    all_gather x1, waiting for transfers between devices, shards(): gram_total = jnp.sum(lax.all_gather(gram_part, 'grid'), axis=0)  329 us
    slice x96, local copies, waits for them, and re-layouts, second_roll(): jnp.roll(values, -reach, along)  137 us
    add x4, other arithmetic, shards(): own_part = local_part + spread[6:6 + slab_planes]  72.9 us
    all_gather x1, waiting for transfers between devices, shards(): piece = lax.all_gather(current, 'band', axis=3, tiled=True)  45.7 us
    ppermute x4, waiting for transfers between devices, padded(): before = lax.ppermute(last, axis, up)  29.3 us
    ppermute x4, starting transfers between devices, padded(): after = lax.ppermute(initial, axis, down)  26.8 us
    ppermute x8, starting transfers between devices, shifted(): lax.ppermute(array, axis, [(i, (i + by) % peers) for i in range(peers)])  25.9 us
    dot_general x4, matrix products, shards(): lax.dot_general(projector_map, correlation, (((0,), (0,)), ((), ())), pre...  20.3 us
  transfers between devices with their start and end apart: 18, of which 6 were waited for; matrix products, arithmetic and copies ran while one was open for 17% of the time, Pallas kernels for 0%

profile of v1, /device:TPU:4, one launch (start us, length us, event | category | flops | bytes accessed | tf_op | source)
XLA Modules:
  0.0 771.0 jit_solution(2904608791884800853)
XLA Ops:
  7.2 2.8 fusion.325
  11.6 7.4 collective-permute-start
  37.5 1.9 fusion.321
  39.3 1.8 fusion.323
  41.2 2.0 fusion.305
  43.2 2.0 fusion.307
  45.2 2.0 fusion.303
  47.2 2.0 fusion.309
  52.9 2.0 fusion.301
  54.8 2.0 fusion.311
  60.2 5.1 fusion.326
  70.2 6.2 collective-permute-start.3
  77.7 14.2 %fusion.105 = f32[12,16,16,128]{3,2,1,0:T(8,128)S(1)} fusion(f32[12,16,16,128]{3,2,1,0:T(8,128)S(1)} %bitcast.62, f32[18,16,16,128]{3,2,1,0:T(8,128)S(1)} %get-tuple-element.305, f32[18,16,16,128]{3,2,1,0:T(8,128)S(1)} %constant_dynamic-update-slice_fusion, f32[12,15,16,128]{3,2,1,0:T(8,128)} %get-tuple-element.301, ...), kind=kLoop, calls=%fused_computation.176 | loop fusion | flops 33423360 | bytes 61353984 | tf_op jit(solution)/shard_map/add | solution.py:102
  91.9 1.8 collective-permute-done.2
  114.5 1.9 fusion.296
  116.4 1.8 fusion.298
  118.3 2.1 fusion.282
  120.4 2.0 fusion.276
  122.4 2.1 fusion.284
  124.5 2.1 fusion.280
  126.6 6.4 collective-permute-start.4
  133.7 2.0 fusion.286
  135.7 2.0 fusion.278
  137.7 11.2 %collective-permute-done.5 = f32[6,16,16,128]{3,2,1,0:T(8,128)S(1)} collective-permute-done((f32[6,16,16,128]{3,2,1,0:T(8,128)S(1)}, f32[6,16,16,128]{3,2,1,0:T(8,128)S(1)}, u32[]{:S(2)}, u32[]{:S(2)}) %collective-permute-start.5) | collective-permute-done | bytes 786464 | tf_op jit(solution)/shard_map/ppermute | solution.py:29
  151.6 5.1 fusion.327
  159.2 6.6 collective-permute-start.7
  165.8 20.1 %fusion.71 = f32[12,16,16,128]{3,2,1,0:T(8,128)} fusion(f32[12,16,16,128]{3,2,1,0:T(8,128)} %bitcast.63, f32[12,16,16,128]{3,2,1,0:T(8,128)S(1)} %broadcast_multiply_fusion, f32[6,16,16,128]{3,2,1,0:T(8,128)S(1)} %collective-permute-done.5, f32[6,16,16,128]{3,2,1,0:T(8,128)} %copy-done.9, f32[12,15,16,128]{3,2,1,0:T(8,128)} %get-tuple-element.251, ...), kind=kLoop, calls=%fused_computation.135 | loop fusion | flops 38928384 | bytes 47198208 | tf_op jit(solution)/shard_map/add | solution.py:102
  185.9 2.4 fusion.215
  188.2 2.4 fusion.214
  190.6 1.9 multiply_subtract_fusion.2
  210.3 1.9 fusion.271
  212.2 1.8 fusion.273
  214.1 2.0 fusion.257
  216.1 2.0 fusion.253
  218.0 2.0 fusion.251
  220.0 2.0 fusion.259
  222.0 6.4 collective-permute-start.8
  229.1 2.0 fusion.261
  231.1 2.0 fusion.255
  233.1 9.9 %collective-permute-done.9 = f32[6,16,16,128]{3,2,1,0:T(8,128)S(1)} collective-permute-done((f32[6,16,16,128]{3,2,1,0:T(8,128)S(1)}, f32[6,16,16,128]{3,2,1,0:T(8,128)S(1)}, u32[]{:S(2)}, u32[]{:S(2)}) %collective-permute-start.9) | collective-permute-done | bytes 786464 | tf_op jit(solution)/shard_map/ppermute | solution.py:29
  245.6 5.1 fusion.328
  252.1 6.4 collective-permute-start.11
  258.6 19.8 %fusion.40 = f32[12,16,16,128]{3,2,1,0:T(8,128)} fusion(f32[12,16,16,128]{3,2,1,0:T(8,128)S(1)} %bitcast.64, f32[12,16,16,128]{3,2,1,0:T(8,128)S(1)} %multiply_subtract_fusion.2, f32[6,16,16,128]{3,2,1,0:T(8,128)S(1)} %collective-permute-done.9, f32[6,16,16,128]{3,2,1,0:T(8,128)} %copy-done.11, f32[12,15,16,128]{3,2,1,0:T(8,128)} %get-tuple-element.201, ...), kind=kLoop, calls=%fused_computation.104 | loop fusion | flops 38141952 | bytes 44052480 | tf_op jit(solution)/shard_map/add | solution.py:102
  278.4 2.3 fusion.213
  280.7 2.4 fusion.212
  283.1 2.0 multiply_subtract_fusion.1
  301.6 1.8 fusion.244
  303.4 1.9 fusion.246
  305.2 1.9 fusion.248
  307.1 2.0 fusion.232
  309.2 2.0 fusion.226
  311.2 2.0 fusion.234
  313.2 2.0 fusion.230
  315.2 6.6 collective-permute-start.12
  322.6 2.0 fusion.236
  324.6 2.0 fusion.228
  326.6 8.2 %collective-permute-done.13 = f32[6,16,16,128]{3,2,1,0:T(8,128)S(1)} collective-permute-done((f32[6,16,16,128]{3,2,1,0:T(8,128)S(1)}, f32[6,16,16,128]{3,2,1,0:T(8,128)S(1)}, u32[]{:S(2)}, u32[]{:S(2)}) %collective-permute-start.13) | collective-permute-done | bytes 786464 | tf_op jit(solution)/shard_map/ppermute | solution.py:29
  337.4 5.1 fusion.329
  343.9 6.5 collective-permute-start.15
  350.4 18.8 %fusion.9 = f32[12,16,16,128]{3,2,1,0:T(8,128)S(1)} fusion(f32[12,16,16,128]{3,2,1,0:T(8,128)S(1)} %bitcast.65, f32[12,16,16,128]{3,2,1,0:T(8,128)S(1)} %multiply_subtract_fusion.1, f32[6,16,16,128]{3,2,1,0:T(8,128)S(1)} %collective-permute-done.13, f32[6,16,16,128]{3,2,1,0:T(8,128)} %copy-done.10, f32[12,15,16,128]{3,2,1,0:T(8,128)} %get-tuple-element.151, ...), kind=kLoop, calls=%fused_computation.73 | loop fusion | flops 38141952 | bytes 44052480 | tf_op jit(solution)/shard_map/add | solution.py:102
  373.4 45.7 %all-gather.4.cloned.1.call-done = f32[12,16,16,512]{3,2,1,0:T(8,128)} async-done(((f32[12,16,16,128]{3,2,1,0:T(8,128)}), f32[12,16,16,512]{3,2,1,0:T(8,128)}) %all-gather.4.cloned.1.call-update) | async-done | bytes 6291472 | tf_op jit(solution)/shard_map/all_gather | solution.py:114
  419.2 7.3 convolution_bitcast_fusion.1
  426.5 329.2 %all-gather.6.cloned.1.call-done = f32[8192,512]{1,0:T(8,128)} async-done(((f32[128,512]{1,0:T(8,128)}), f32[8192,512]{1,0:T(8,128)}) %all-gather.6.cloned.1.call-update) | async-done | bytes 16777232 | tf_op jit(solution)/shard_map/all_gather | solution.py:118
  755.7 7.6 reduce_sum.9
  (156 shorter events, 108.5 us)
Async XLA Ops:
  7.2 42.1 %copy-start = (f32[4,8,13,256]{3,1,2,0:T(8,128)S(1)}, f32[4,8,13,256]{3,1,2,0:T(8,128)}, u32[]{:S(2)}) copy-start(f32[4,8,13,256]{3,1,2,0:T(8,128)} %param.23) | copy-start | bytes 1277956
  7.2 11.8 %copy-start.2 = (f32[12,16,16,128]{3,2,1,0:T(8,128)S(1)}, f32[12,16,16,128]{3,2,1,0:T(8,128)}, u32[]{:S(2)}) copy-start(f32[12,16,16,128]{3,2,1,0:T(8,128)} %param.21) | copy-start | bytes 4718596
  7.2 412.0 %all-gather.4.cloned.1.call-start = ((), (), s32[]{:S(2)}) async-start(), calls=%async_computation | async-start | bytes 7864320 | tf_op jit(solution)/shard_map/all_gather | solution.py:114
  10.0 46.8 %collective-permute-start.1 = (f32[6,16,16,128]{3,2,1,0:T(8,128)}, f32[6,16,16,128]{3,2,1,0:T(8,128)}, u32[]{:S(2)}, u32[]{:S(2)}) collective-permute-start(f32[6,16,16,128]{3,2,1,0:T(8,128)} %get-tuple-element.306), channel_id=1, source_target_pairs={{0,1},{1,2},{2,3},{3,4},{4,5},{5,6},{6,7},{7,8},{8,9},{9,10},{10,1... | collective-permute-start | bytes 2359304 | tf_op jit(solution)/shard_map/ppermute | solution.py:29
  11.6 45.2 %collective-permute-start = (f32[6,16,16,128]{3,2,1,0:T(8,128)}, f32[6,16,16,128]{3,2,1,0:T(8,128)}, u32[]{:S(2)}, u32[]{:S(2)}) collective-permute-start(f32[6,16,16,128]{3,2,1,0:T(8,128)} %get-tuple-element.307), channel_id=1, source_target_pairs={{1,0},{2,1},{3,2},{4,3},{5,4},{6,5},{7,6},{8,7},{9,8},{10,9},{11,1... | collective-permute-start | bytes 2359304 | tf_op jit(solution)/shard_map/ppermute | solution.py:30
  47.2 2.1 copy-start.15
  47.2 3.6 copy-start.14
  47.2 4.2 copy-start.16
  65.3 1.7 copy-start.4
  68.3 9.3 %copy-start.12 = (f32[12,16,5,128]{3,2,1,0:T(8,128)S(1)}, f32[12,16,5,128]{3,2,1,0:T(8,128)}, u32[]{:S(2)}) copy-start(f32[12,16,5,128]{3,2,1,0:T(8,128)} %get-tuple-element.262) | copy-start | bytes 1474564
  68.3 9.3 %copy-start.13 = (f32[12,16,3,128]{3,2,1,0:T(4,128)S(1)}, f32[12,16,3,128]{3,2,1,0:T(4,128)}, u32[]{:S(2)}) copy-start(f32[12,16,3,128]{3,2,1,0:T(4,128)} %get-tuple-element.270) | copy-start | bytes 884740
  69.6 8.1 %copy-start.5 = (f32[12,16,12,128]{3,2,1,0:T(8,128)S(1)}, f32[12,16,12,128]{3,2,1,0:T(8,128)}, u32[]{:S(2)}) copy-start(f32[12,16,12,128]{3,2,1,0:T(8,128)} %get-tuple-element.264) | copy-start | bytes 3538948
  69.6 8.1 %copy-start.6 = (f32[12,16,12,128]{3,2,1,0:T(8,128)S(1)}, f32[12,16,12,128]{3,2,1,0:T(8,128)}, u32[]{:S(2)}) copy-start(f32[12,16,12,128]{3,2,1,0:T(8,128)} %get-tuple-element.265) | copy-start | bytes 3538948
  69.6 8.1 %copy-start.7 = (f32[12,16,13,128]{3,2,1,0:T(8,128)S(1)}, f32[12,16,13,128]{3,2,1,0:T(8,128)}, u32[]{:S(2)}) copy-start(f32[12,16,13,128]{3,2,1,0:T(8,128)} %get-tuple-element.268) | copy-start | bytes 3833860
  70.1 7.6 slice-start
  70.1 23.6 %collective-permute-start.2 = (f32[6,16,16,128]{3,2,1,0:T(8,128)}, f32[6,16,16,128]{3,2,1,0:T(8,128)}, u32[]{:S(2)}, u32[]{:S(2)}) collective-permute-start(f32[6,16,16,128]{3,2,1,0:T(8,128)} %bitcast.5), channel_id=1, source_target_pairs={{0,1},{1,2},{2,3},{3,4},{4,5},{5,6},{6,7},{7,8},{8,9},{9,10},{10,1... | collective-permute-start | bytes 2359304 | tf_op jit(solution)/shard_map/ppermute | solution.py:37
  70.2 24.9 %collective-permute-start.3 = (f32[6,16,16,128]{3,2,1,0:T(8,128)}, f32[6,16,16,128]{3,2,1,0:T(8,128)}, u32[]{:S(2)}, u32[]{:S(2)}) collective-permute-start(f32[6,16,16,128]{3,2,1,0:T(8,128)} %bitcast.6), channel_id=1, source_target_pairs={{0,63},{1,0},{2,1},{3,2},{4,3},{5,4},{6,5},{7,6},{8,7},{9,8},{10,9... | collective-permute-start | bytes 2359304 | tf_op jit(solution)/shard_map/ppermute | solution.py:37
  126.6 22.4 %collective-permute-start.5 = (f32[6,16,16,128]{3,2,1,0:T(8,128)S(1)}, f32[6,16,16,128]{3,2,1,0:T(8,128)S(1)}, u32[]{:S(2)}, u32[]{:S(2)}) collective-permute-start(f32[6,16,16,128]{3,2,1,0:T(8,128)S(1)} %get-tuple-element.254), channel_id=1, source_target_pairs={{0,1},{1,2},{2,3},{3,4},{4,5},{5,6},{6,7},{7,8},{8,9},{9,10},{10,1... | collective-permute-start | bytes 2359304 | tf_op jit(solution)/shard_map/ppermute | solution.py:29
  126.6 22.4 %collective-permute-start.4 = (f32[6,16,16,128]{3,2,1,0:T(8,128)S(1)}, f32[6,16,16,128]{3,2,1,0:T(8,128)S(1)}, u32[]{:S(2)}, u32[]{:S(2)}) collective-permute-start(f32[6,16,16,128]{3,2,1,0:T(8,128)S(1)} %get-tuple-element.255), channel_id=1, source_target_pairs={{1,0},{2,1},{3,2},{4,3},{5,4},{6,5},{7,6},{8,7},{9,8},{10,9},{11,1... | collective-permute-start | bytes 2359304 | tf_op jit(solution)/shard_map/ppermute | solution.py:30
  148.9 1.0 copy-start.9
  159.2 26.7 %collective-permute-start.6 = (f32[6,16,16,128]{3,2,1,0:T(8,128)}, f32[6,16,16,128]{3,2,1,0:T(8,128)}, u32[]{:S(2)}, u32[]{:S(2)}) collective-permute-start(f32[6,16,16,128]{3,2,1,0:T(8,128)} %bitcast.9), channel_id=1, source_target_pairs={{0,1},{1,2},{2,3},{3,4},{4,5},{5,6},{6,7},{7,8},{8,9},{9,10},{10,1... | collective-permute-start | bytes 2359304 | tf_op jit(solution)/shard_map/ppermute | solution.py:37
  159.2 29.1 %collective-permute-start.7 = (f32[6,16,16,128]{3,2,1,0:T(8,128)}, f32[6,16,16,128]{3,2,1,0:T(8,128)}, u32[]{:S(2)}, u32[]{:S(2)}) collective-permute-start(f32[6,16,16,128]{3,2,1,0:T(8,128)} %bitcast.10), channel_id=1, source_target_pairs={{0,63},{1,0},{2,1},{3,2},{4,3},{5,4},{6,5},{7,6},{8,7},{9,8},{10,9... | collective-permute-start | bytes 2359304 | tf_op jit(solution)/shard_map/ppermute | solution.py:37
  222.0 20.9 %collective-permute-start.9 = (f32[6,16,16,128]{3,2,1,0:T(8,128)S(1)}, f32[6,16,16,128]{3,2,1,0:T(8,128)S(1)}, u32[]{:S(2)}, u32[]{:S(2)}) collective-permute-start(f32[6,16,16,128]{3,2,1,0:T(8,128)S(1)} %get-tuple-element.204), channel_id=1, source_target_pairs={{0,1},{1,2},{2,3},{3,4},{4,5},{5,6},{6,7},{7,8},{8,9},{9,10},{10,1... | collective-permute-start | bytes 2359304 | tf_op jit(solution)/shard_map/ppermute | solution.py:29
  222.0 20.9 %collective-permute-start.8 = (f32[6,16,16,128]{3,2,1,0:T(8,128)S(1)}, f32[6,16,16,128]{3,2,1,0:T(8,128)S(1)}, u32[]{:S(2)}, u32[]{:S(2)}) collective-permute-start(f32[6,16,16,128]{3,2,1,0:T(8,128)S(1)} %get-tuple-element.205), channel_id=1, source_target_pairs={{1,0},{2,1},{3,2},{4,3},{5,4},{6,5},{7,6},{8,7},{9,8},{10,9},{11,1... | collective-permute-start | bytes 2359304 | tf_op jit(solution)/shard_map/ppermute | solution.py:30
  243.0 0.9 copy-start.11
  252.1 26.2 %collective-permute-start.10 = (f32[6,16,16,128]{3,2,1,0:T(8,128)}, f32[6,16,16,128]{3,2,1,0:T(8,128)}, u32[]{:S(2)}, u32[]{:S(2)}) collective-permute-start(f32[6,16,16,128]{3,2,1,0:T(8,128)} %bitcast.13), channel_id=1, source_target_pairs={{0,1},{1,2},{2,3},{3,4},{4,5},{5,6},{6,7},{7,8},{8,9},{9,10},{10,1... | collective-permute-start | bytes 2359304 | tf_op jit(solution)/shard_map/ppermute | solution.py:37
  252.1 28.6 %collective-permute-start.11 = (f32[6,16,16,128]{3,2,1,0:T(8,128)}, f32[6,16,16,128]{3,2,1,0:T(8,128)}, u32[]{:S(2)}, u32[]{:S(2)}) collective-permute-start(f32[6,16,16,128]{3,2,1,0:T(8,128)} %bitcast.14), channel_id=1, source_target_pairs={{0,63},{1,0},{2,1},{3,2},{4,3},{5,4},{6,5},{7,6},{8,7},{9,8},{10,9... | collective-permute-start | bytes 2359304 | tf_op jit(solution)/shard_map/ppermute | solution.py:37
  315.2 19.5 %collective-permute-start.13 = (f32[6,16,16,128]{3,2,1,0:T(8,128)S(1)}, f32[6,16,16,128]{3,2,1,0:T(8,128)S(1)}, u32[]{:S(2)}, u32[]{:S(2)}) collective-permute-start(f32[6,16,16,128]{3,2,1,0:T(8,128)S(1)} %get-tuple-element.154), channel_id=1, source_target_pairs={{0,1},{1,2},{2,3},{3,4},{4,5},{5,6},{6,7},{7,8},{8,9},{9,10},{10,1... | collective-permute-start | bytes 2359304 | tf_op jit(solution)/shard_map/ppermute | solution.py:29
  315.2 19.5 %collective-permute-start.12 = (f32[6,16,16,128]{3,2,1,0:T(8,128)S(1)}, f32[6,16,16,128]{3,2,1,0:T(8,128)S(1)}, u32[]{:S(2)}, u32[]{:S(2)}) collective-permute-start(f32[6,16,16,128]{3,2,1,0:T(8,128)S(1)} %get-tuple-element.155), channel_id=1, source_target_pairs={{1,0},{2,1},{3,2},{4,3},{5,4},{6,5},{7,6},{8,7},{9,8},{10,9},{11,1... | collective-permute-start | bytes 2359304 | tf_op jit(solution)/shard_map/ppermute | solution.py:30
  334.8 0.9 copy-start.10
  342.6 7.7 %copy-start.8 = (f32[12,12,16,128]{3,2,1,0:T(8,128)S(1)}, f32[12,12,16,128]{3,2,1,0:T(8,128)}, u32[]{:S(2)}) copy-start(f32[12,12,16,128]{3,2,1,0:T(8,128)} %get-tuple-element.138) | copy-start | bytes 3538948
  343.9 25.3 %collective-permute-start.14 = (f32[6,16,16,128]{3,2,1,0:T(8,128)}, f32[6,16,16,128]{3,2,1,0:T(8,128)}, u32[]{:S(2)}, u32[]{:S(2)}) collective-permute-start(f32[6,16,16,128]{3,2,1,0:T(8,128)} %bitcast.17), channel_id=1, source_target_pairs={{0,1},{1,2},{2,3},{3,4},{4,5},{5,6},{6,7},{7,8},{8,9},{9,10},{10,1... | collective-permute-start | bytes 2359304 | tf_op jit(solution)/shard_map/ppermute | solution.py:37
  343.9 26.7 %collective-permute-start.15 = (f32[6,16,16,128]{3,2,1,0:T(8,128)}, f32[6,16,16,128]{3,2,1,0:T(8,128)}, u32[]{:S(2)}, u32[]{:S(2)}) collective-permute-start(f32[6,16,16,128]{3,2,1,0:T(8,128)} %bitcast.18), channel_id=1, source_target_pairs={{0,63},{1,0},{2,1},{3,2},{4,3},{5,4},{6,5},{7,6},{8,7},{9,8},{10,9... | collective-permute-start | bytes 2359304 | tf_op jit(solution)/shard_map/ppermute | solution.py:37
  373.4 45.8 %copy-start.3 = (f32[12,16,16,128]{3,2,1,0:T(8,128)S(1)}, f32[12,16,16,128]{3,2,1,0:T(8,128)}, u32[]{:S(2)}) copy-start(f32[12,16,16,128]{3,2,1,0:T(8,128)} %multiply_subtract_fusion) | copy-start | bytes 4718596
  373.4 382.3 %all-gather.6.cloned.1.call-start = ((), (), s32[]{:S(2)}) async-start(), calls=%async_computation.1 | async-start | bytes 17039360 | tf_op jit(solution)/shard_map/all_gather | solution.py:118
  755.7 8.3 %copy-start.1 = (f32[4,8,13,256]{3,1,2,0:T(8,128)S(1)}, f32[4,8,13,256]{3,1,2,0:T(8,128)}, u32[]{:S(2)}) copy-start(f32[4,8,13,256]{3,1,2,0:T(8,128)} %param.23) | copy-start | bytes 1277956
Sparse Core Ops, SparseCore 0:
  373.5 45.6 all-gather.3
  426.6 329.0 all-gather.5
